TPU v7x, 32 devices: a whole 2x2x4 slice. The times are simulated.
32 devices in a mesh: groups: 2 (over x), seq: 16 (over z, y, core).
Axes of the slice: x: 2, y: 2, z: 4, core: 2. Of those that a mesh axis runs over, the one named last changes fastest.
Arguments:
- hidden: bfloat16 [16384, 320], P(('groups', 'seq')), parts along dimension 0, may hold values from -20 to 20
- ref_hidden: bfloat16 [2048, 320], P(('groups', 'seq')), parts along dimension 0, may hold values from -6 to 6
- visible: int32 [128, 64], P('groups'), parts along dimension 0, may hold values 0 or 1
- ref_count: int32 [2], P('groups'), parts along dimension 0, may hold values from 256 to 1024
- w_query: bfloat16 [320, 320], replicated, may hold values from -0.3125 to 0.3125
- w_key: bfloat16 [320, 320], replicated, may hold values from -0.3125 to 0.3125
- w_value: bfloat16 [320, 320], replicated, may hold values from -0.3125 to 0.3125
- w_out: bfloat16 [320, 320], replicated, may hold values from -0.3125 to 0.3125
Outputs:
- attended: bfloat16 [16384, 320], P(('groups', 'seq')), parts along dimension 0
There are 2 independent parts, one for each index of `groups`. A program takes and returns all parts, laid end to end along the dimension named above; an argument that names none is the same for every part. Nothing has to cross between parts.
All inputs are finite; a program needn't handle non-finite values.
Results may differ from a plain program's by a relative error of at most 0.011.
Values may be sent and summed in bfloat16 or wider, within the bound.
A program may use at most 128 MiB of HBM per device.

v0:
```python
import math
import jax
import jax.numpy as jnp
from jax import lax
from jax.sharding import PartitionSpec as P

HEADS = 5
TILE = 128
TILES_VIEW = 8


def project(states, weight, head_count):
    result = jnp.dot(states, weight, preferred_element_type=jnp.float32).astype(jnp.bfloat16)
    return result.reshape(states.shape[0], head_count, weight.shape[1] // head_count)


def local(hidden, ref_hidden, visible, ref_count, w_query, w_key, w_value, w_out):
    row_count = hidden.shape[0]
    width = hidden.shape[1]
    head_count = HEADS
    head_size = width // head_count
    scale = 1.0 / math.sqrt(head_size)
    tile_count = visible.shape[0]
    view_tiles = TILES_VIEW
    row_start = lax.axis_index("seq") * row_count
    queries = project(hidden, w_query, head_count)
    row_tile = (row_start + jnp.arange(row_count, dtype=jnp.int32)) // TILE
    row_view = row_tile // view_tiles
    picker = (row_tile[:, None] == jnp.arange(tile_count, dtype=jnp.int32)[None, :]).astype(
        jnp.float32
    )
    seen_tiles = jnp.dot(picker, visible.astype(jnp.float32))

    def attend(state, key_rows, value_rows, allowed):
        run_max, run_total, run_acc = state
        scores = (
            jnp.einsum("qhd,khd->hqk", queries, key_rows, preferred_element_type=jnp.float32)
            * scale
        )
        scores = jnp.where(allowed[None, :, :], scores, jnp.float32(-1e30))
        new_max = jnp.maximum(run_max, jnp.max(scores, axis=-1))
        expo = jnp.exp(scores - new_max[:, :, None])
        factor = jnp.exp(run_max - new_max)
        new_total = run_total * factor + jnp.sum(expo, axis=-1)
        new_acc = run_acc * factor[:, :, None] + jnp.einsum(
            "hqk,khd->hqd",
            expo.astype(jnp.bfloat16),
            value_rows,
            preferred_element_type=jnp.float32,
        )
        return (new_max, new_total, new_acc)

    def view_block(state, key_rows, value_rows, offset):
        key_count = key_rows.shape[0]
        key_tile = (offset + jnp.arange(key_count, dtype=jnp.int32)) // TILE
        onehot = (key_tile[:, None] == jnp.arange(tile_count, dtype=jnp.int32)[None, :]).astype(
            jnp.float32
        )
        tile_hits = jnp.dot(seen_tiles, onehot.T)
        allowed = (tile_hits > 0.5) | (row_view[:, None] == (key_tile // view_tiles)[None, :])
        return attend(state, key_rows, value_rows, allowed)

    local_keys = jnp.dot(ref_hidden, w_key, preferred_element_type=jnp.float32).astype(jnp.bfloat16)
    local_values = jnp.dot(ref_hidden, w_value, preferred_element_type=jnp.float32).astype(
        jnp.bfloat16
    )
    ref_keys, ref_values = (
        lax.all_gather(local_keys, "seq", axis=0, tiled=True),
        lax.all_gather(local_values, "seq", axis=0, tiled=True),
    )
    ref_keys = ref_keys.reshape(ref_keys.shape[0], head_count, head_size)
    ref_values = ref_values.reshape(ref_values.shape[0], head_count, head_size)
    ref_total = ref_keys.shape[0]
    ref_allowed = jnp.broadcast_to(
        (jnp.arange(ref_total, dtype=jnp.int32) < ref_count[0])[None, :], (row_count, ref_total)
    )
    initial = (
        jnp.full((head_count, row_count), -1e30, jnp.float32),
        jnp.zeros((head_count, row_count), jnp.float32),
        jnp.zeros((head_count, row_count, head_size), jnp.float32),
    )
    state = attend(initial, ref_keys, ref_values, ref_allowed)
    view_keys = project(hidden, w_key, head_count)
    view_values = project(hidden, w_value, head_count)
    pieces = (
        lax.all_gather(view_keys, "seq", axis=0, tiled=True),
        lax.all_gather(view_values, "seq", axis=0, tiled=True),
    )
    sweep_state = state
    key_rows = pieces[0]
    value_rows = pieces[1]
    key_count = key_rows.shape[0]
    block_size = 512
    block_count = key_count // block_size
    key_blocks = key_rows.reshape(block_count, block_size, head_count, head_size)
    value_blocks = value_rows.reshape(block_count, block_size, head_count, head_size)

    def advance(inner, pieces):
        block_index, key_part, value_part = pieces
        return (view_block(inner, key_part, value_part, block_index * block_size), None)

    sweep_state, unused = lax.scan(
        advance, sweep_state, (jnp.arange(block_count, dtype=jnp.int32), key_blocks, value_blocks)
    )
    state = sweep_state
    run_max, run_total, run_acc = state
    mixed = run_acc / run_total[:, :, None]
    mixed = jnp.transpose(mixed, (1, 0, 2)).reshape(row_count, width).astype(jnp.bfloat16)
    return jnp.dot(mixed, w_out, preferred_element_type=jnp.float32).astype(jnp.bfloat16)


def solution(mesh):
    in_specs = (
        P(("groups", "seq"), None),
        P(("groups", "seq"), None),
        P("groups", None),
        P("groups"),
        P(),
        P(),
        P(),
        P(),
    )
    out_specs = P(("groups", "seq"), None)
    return jax.shard_map(local, mesh=mesh, in_specs=in_specs, out_specs=out_specs, check_vma=False)
```

profile of v0, /device:TPU:0, one launch (start us, length us, event | category | flops | bytes accessed | tf_op | source)
XLA Modules:
  0.0 273.2 jit_solution(13204093446191117111)
XLA Ops:
  13.5 28.4 %all_gather.12 = bf16[1024,320]{1,0:T(8,128)(2,1)S(1)} all-gather(bf16[64,320]{1,0:T(8,128)(2,1)S(1)} %convolution_convert_fusion.5), channel_id=1, replica_groups=mesh['groups'=2,'seq'=16] {'seq'}, dimensions={0}, use_global_device_ids=true | all-gather | bytes 696320 | tf_op jit(solution)/shard_map/all_gather | solution.py:68
  43.3 24.3 %all_gather.13 = bf16[1024,320]{1,0:T(8,128)(2,1)S(1)} all-gather(bf16[64,320]{1,0:T(8,128)(2,1)S(1)} %convolution_convert_fusion.4), channel_id=1, replica_groups=mesh['groups'=2,'seq'=16] {'seq'}, dimensions={0}, use_global_device_ids=true | all-gather | bytes 696320 | tf_op jit(solution)/shard_map/all_gather | solution.py:69
  69.9 2.5 fusion.35
  75.0 4.0 %all-gather.5.cloned.1.call-done = bf16[8192,5,64]{0,2,1:T(8,128)(2,1)} async-done(((bf16[512,5,64]{0,2,1:T(8,128)(2,1)}), bf16[8192,5,64]{0,2,1:T(8,128)(2,1)}) %all-gather.5.cloned.1.call-update) | async-done | bytes 5242896 | tf_op jit(solution)/shard_map/all_gather | solution.py:87
  79.0 5.6 %copy.25 = bf16[5,8,16,8,512]{4,3,1,0,2:T(8,128)(2,1)} copy(bf16[5,8,16,8,512]{4,3,2,1,0:T(8,128)(2,1)} %bitcast.81) | data formatting | bytes 10485760 | tf_op jit(solution)/shard_map/reshape | solution.py:96
  84.6 56.0 %all-gather.3.cloned.1.call-done = bf16[8192,5,64]{0,2,1:T(8,128)(2,1)} async-done(((bf16[512,5,64]{0,2,1:T(8,128)(2,1)}), bf16[8192,5,64]{0,2,1:T(8,128)(2,1)}) %all-gather.3.cloned.1.call-update) | async-done | bytes 5242896 | tf_op jit(solution)/shard_map/all_gather | solution.py:86
  140.6 5.6 %copy.26 = bf16[5,8,16,8,512]{4,3,1,0,2:T(8,128)(2,1)} copy(bf16[5,8,16,8,512]{4,3,2,1,0:T(8,128)(2,1)} %bitcast.82) | data formatting | bytes 10485760 | tf_op jit(solution)/shard_map/reshape | solution.py:95
  146.2 118.9 %while.18 = (s32[]{:T(128)}, f32[5,512]{1,0:T(8,128)S(1)}, f32[5,512]{1,0:T(8,128)S(1)}, f32[5,512,64]{1,2,0:T(8,128)S(1)}, s32[16]{0:T(128)S(1)}, /*index=5*/bf...) while((s32[]{:T(128)}, f32[5,512]{1,0:T(8,128)S(1)}, ...), condition=%wide.region_5.6_spmd.clone, body=%wide.region_2.5_spmd.clone.sunk | while | flops 384700416 | bytes 19313812 | solution.py:102
  151.1 2.5 fusion.83
  158.5 2.5 fusion.83
  166.0 2.5 fusion.83
  173.4 2.5 fusion.83
  180.8 2.5 fusion.83
  188.3 2.5 fusion.83
  195.7 2.5 fusion.83
  203.1 2.5 fusion.83
  210.6 2.5 fusion.83
  218.0 2.5 fusion.83
  225.4 2.5 fusion.83
  232.9 2.5 fusion.83
  240.3 2.5 fusion.83
  247.7 2.5 fusion.83
  255.2 2.5 fusion.83
  262.6 2.5 fusion.83
  (173 shorter events, 80.5 us)
Async XLA Ops:
  6.5 1.0 copy-start
  6.5 61.3 %copy-start.1 = (bf16[320,320]{1,0:T(8,128)(2,1)S(1)}, bf16[320,320]{1,0:T(8,128)(2,1)}, u32[]{:S(2)}) copy-start(bf16[320,320]{1,0:T(8,128)(2,1)} %param.14) | copy-start | bytes 614404
  6.5 72.5 %all-gather.5.cloned.1.call-start = ((), (), s32[]{:S(2)}) async-start(), calls=%async_computation.1 | async-start | bytes 5570560 | tf_op jit(solution)/shard_map/all_gather | solution.py:87
  9.6 131.1 %all-gather.3.cloned.1.call-start = ((), (), s32[]{:S(2)}) async-start(), calls=%async_computation | async-start | bytes 5570560 | tf_op jit(solution)/shard_map/all_gather | solution.py:86
  69.9 2.5 copy-start.3
  146.2 119.0 %copy-start.2 = (bf16[320,320]{1,0:T(8,128)(2,1)S(1)}, bf16[320,320]{1,0:T(8,128)(2,1)}, u32[]{:S(2)}) copy-start(bf16[320,320]{1,0:T(8,128)(2,1)} %param.17) | copy-start | bytes 614404
Sparse Core Ops, SparseCore 0:
  9.7 69.3 all-gather.4
  81.2 59.3 all-gather.2
where the time goes:
time: 275 us; the launch traced here: 273 us
  matrix products  91.4 us (33%)
  waiting for transfers between devices  60.1 us (22%)
  blocking collectives  52.6 us (19%)
  local copies, waits for them, and re-layouts  22.1 us (8%)
  other arithmetic  21.1 us (8%)
  between operations  14.2 us (5%)
  loops' own time  11.7 us (4%)
    all_gather x1, waiting for transfers between devices, local(): lax.all_gather(view_keys, 'seq', axis=0, tiled=True)  56 us
    dot_general x17, matrix products, attend(): jnp.einsum('hqk,khd->hqd', expo.astype(jnp.bfloat16), value_rows, preferr...  42.9 us
    dot_general x17, matrix products, attend(): jnp.einsum('qhd,khd->hqk', queries, key_rows, preferred_element_type=jnp....  34.2 us
    all_gather x1, blocking collectives, local(): lax.all_gather(local_keys, 'seq', axis=0, tiled=True)  28.4 us
    all_gather x1, blocking collectives, local(): lax.all_gather(local_values, 'seq', axis=0, tiled=True)  24.3 us
    reduce_sum x17, other arithmetic, attend(): new_total = run_total * factor + jnp.sum(expo, axis=-1)  20.1 us
    another operation x1, loops' own time, local(): lax.scan(advance, sweep_state, (jnp.arange(block_count, dtype=jnp.int32),...  11.7 us
    dynamic_slice x16, local copies, waits for them, and re-layouts, local(): lax.scan(advance, sweep_state, (jnp.arange(block_count, dtype=jnp.int32),...  9.38 us
  transfers between devices with their start and end apart: 2, of which 2 were waited for; matrix products, arithmetic and copies ran while one was open for 6% of the time, Pallas kernels for 0%

commit v1 on v0

--- a/solution.py
+++ b/solution.py
@@ -64,8 +64,23 @@
     local_values = jnp.dot(ref_hidden, w_value, preferred_element_type=jnp.float32).astype(
         jnp.bfloat16
     )
+
+    def rounds_get(s0, shard_axis):
+        parts_out = lax.axis_index(shard_axis)
+        u_next = lax.axis_size(shard_axis)
+        high, next_value, taken_in = (u_next, parts_out, s0.shape[0])
+        later = jnp.zeros((*s0.shape[:0], high * taken_in, *s0.shape[1:]), s0.dtype)
+        val = s0
+        sides = [(i, (i + 1) % high) for i in range(high)]
+        for k in range(high):
+            field_out = (next_value - k) % high
+            later = lax.dynamic_update_slice_in_dim(later, val, field_out * taken_in, axis=0)
+            if k < high - 1:
+                val = lax.ppermute(val, shard_axis, sides)
+        return later
+
     ref_keys, ref_values = (
-        lax.all_gather(local_keys, "seq", axis=0, tiled=True),
+        rounds_get(local_keys, "seq"),
         lax.all_gather(local_values, "seq", axis=0, tiled=True),
     )
     ref_keys = ref_keys.reshape(ref_keys.shape[0], head_count, head_size)

time: 275 us -> 282 us (1.025)
  blocking collectives: 52.6 us -> 22.9 us
  waiting for transfers between devices: 60.1 us -> 83.8 us
  local copies, waits for them, and re-layouts: 22.1 us -> 32.5 us
    ppermute x0 -> x15, waiting for transfers between devices: none -> 83.7 us  [rounds_get(): val = lax.ppermute(val, shard_axis, sides)]
    all_gather x1, waiting for transfers between devices: 56 us -> 0.01 us  [local(): lax.all_gather(view_keys, 'seq', axis=0, tiled=True)]
    all_gather x1 -> x0, blocking collectives: 28.4 us -> none  [local(): lax.all_gather(local_keys, 'seq', axis=0, tiled=True)]
    dynamic_update_slice x0 -> x16, local copies, waits for them, and re-layouts: none -> 8.59 us  [rounds_get(): lax.dynamic_update_slice_in_dim(later, val, field_out * taken_in, axis=0)]
    all_gather x1, waiting for transfers between devices: 4.02 us -> 0.02 us  [local(): lax.all_gather(view_values, 'seq', axis=0, tiled=True)]
  transfers between devices with their start and end apart: 2 -> 17, of which waited for: 2 -> 13; matrix products, arithmetic and copies ran while one was open for 6% -> 11% of each run, Pallas kernels for 0% -> 0%
where the time goes in v1:
time: 282 us; the launch traced here: 281 us
  matrix products  93.1 us (33%)
  waiting for transfers between devices  83.8 us (30%)
  local copies, waits for them, and re-layouts  32.5 us (12%)
  blocking collectives  22.9 us (8%)
  other arithmetic  21.1 us (7%)
  between operations  14.7 us (5%)
  loops' own time  11.7 us (4%)
    ppermute x15, waiting for transfers between devices, rounds_get(): val = lax.ppermute(val, shard_axis, sides)  83.7 us
    dot_general x17, matrix products, attend(): jnp.einsum('hqk,khd->hqd', expo.astype(jnp.bfloat16), value_rows, preferr...  42.9 us
    dot_general x17, matrix products, attend(): jnp.einsum('qhd,khd->hqk', queries, key_rows, preferred_element_type=jnp....  34.2 us
    all_gather x1, blocking collectives, local(): lax.all_gather(local_values, 'seq', axis=0, tiled=True)  22.9 us
    reduce_sum x17, other arithmetic, attend(): new_total = run_total * factor + jnp.sum(expo, axis=-1)  20.1 us
    another operation x1, loops' own time, local(): lax.scan(advance, sweep_state, (jnp.arange(block_count, dtype=jnp.int32),...  11.7 us
    dynamic_slice x16, local copies, waits for them, and re-layouts, local(): lax.scan(advance, sweep_state, (jnp.arange(block_count, dtype=jnp.int32),...  9.38 us
    dynamic_update_slice x16, local copies, waits for them, and re-layouts, rounds_get(): lax.dynamic_update_slice_in_dim(later, val, field_out * taken_in, axis=0)  8.59 us
  transfers between devices with their start and end apart: 17, of which 13 were waited for; matrix products, arithmetic and copies ran while one was open for 11% of the time, Pallas kernels for 0%

profile of v1, /device:TPU:0, one launch (start us, length us, event | category | flops | bytes accessed | tf_op | source)
XLA Modules:
  0.0 280.6 jit_solution(7759170977460565810)
XLA Ops:
  13.4 6.8 %collective-permute-done = bf16[64,320]{1,0:T(8,128)(2,1)S(1)} collective-permute-done((bf16[64,320]{1,0:T(8,128)(2,1)S(1)}, bf16[64,320]{1,0:T(8,128)(2,1)S(1)}, u32[]{:S(2)}, u32[]{:S(2)}) %collective-permute-start) | collective-permute-done | bytes 40992 | tf_op jit(solution)/shard_map/ppermute | solution.py:79
  20.1 6.8 %collective-permute-done.1 = bf16[64,320]{1,0:T(8,128)(2,1)S(1)} collective-permute-done((bf16[64,320]{1,0:T(8,128)(2,1)S(1)}, bf16[64,320]{1,0:T(8,128)(2,1)S(1)}, u32[]{:S(2)}, u32[]{:S(2)}) %collective-permute-start.1) | collective-permute-done | bytes 40992 | tf_op jit(solution)/shard_map/ppermute | solution.py:79
  27.0 7.0 %collective-permute-done.2 = bf16[64,320]{1,0:T(8,128)(2,1)S(1)} collective-permute-done((bf16[64,320]{1,0:T(8,128)(2,1)S(1)}, bf16[64,320]{1,0:T(8,128)(2,1)S(1)}, u32[]{:S(2)}, u32[]{:S(2)}) %collective-permute-start.2) | collective-permute-done | bytes 40992 | tf_op jit(solution)/shard_map/ppermute | solution.py:79
  34.0 6.2 %collective-permute-done.3 = bf16[64,320]{1,0:T(8,128)(2,1)S(1)} collective-permute-done((bf16[64,320]{1,0:T(8,128)(2,1)S(1)}, bf16[64,320]{1,0:T(8,128)(2,1)S(1)}, u32[]{:S(2)}, u32[]{:S(2)}) %collective-permute-start.3) | collective-permute-done | bytes 40992 | tf_op jit(solution)/shard_map/ppermute | solution.py:79
  40.2 6.2 %collective-permute-done.4 = bf16[64,320]{1,0:T(8,128)(2,1)S(1)} collective-permute-done((bf16[64,320]{1,0:T(8,128)(2,1)S(1)}, bf16[64,320]{1,0:T(8,128)(2,1)S(1)}, u32[]{:S(2)}, u32[]{:S(2)}) %collective-permute-start.4) | collective-permute-done | bytes 40992 | tf_op jit(solution)/shard_map/ppermute | solution.py:79
  46.4 7.4 %collective-permute-done.5 = bf16[64,320]{1,0:T(8,128)(2,1)S(1)} collective-permute-done((bf16[64,320]{1,0:T(8,128)(2,1)S(1)}, bf16[64,320]{1,0:T(8,128)(2,1)S(1)}, u32[]{:S(2)}, u32[]{:S(2)}) %collective-permute-start.5) | collective-permute-done | bytes 40992 | tf_op jit(solution)/shard_map/ppermute | solution.py:79
  53.8 7.1 %collective-permute-done.6 = bf16[64,320]{1,0:T(8,128)(2,1)S(1)} collective-permute-done((bf16[64,320]{1,0:T(8,128)(2,1)S(1)}, bf16[64,320]{1,0:T(8,128)(2,1)S(1)}, u32[]{:S(2)}, u32[]{:S(2)}) %collective-permute-start.6) | collective-permute-done | bytes 40992 | tf_op jit(solution)/shard_map/ppermute | solution.py:79
  60.9 7.2 %collective-permute-done.7 = bf16[64,320]{1,0:T(8,128)(2,1)S(1)} collective-permute-done((bf16[64,320]{1,0:T(8,128)(2,1)S(1)}, bf16[64,320]{1,0:T(8,128)(2,1)S(1)}, u32[]{:S(2)}, u32[]{:S(2)}) %collective-permute-start.7) | collective-permute-done | bytes 40992 | tf_op jit(solution)/shard_map/ppermute | solution.py:79
  68.2 6.2 %collective-permute-done.8 = bf16[64,320]{1,0:T(8,128)(2,1)S(1)} collective-permute-done((bf16[64,320]{1,0:T(8,128)(2,1)S(1)}, bf16[64,320]{1,0:T(8,128)(2,1)S(1)}, u32[]{:S(2)}, u32[]{:S(2)}) %collective-permute-start.8) | collective-permute-done | bytes 40992 | tf_op jit(solution)/shard_map/ppermute | solution.py:79
  75.5 5.1 %collective-permute-done.9 = bf16[64,320]{1,0:T(8,128)(2,1)S(1)} collective-permute-done((bf16[64,320]{1,0:T(8,128)(2,1)S(1)}, bf16[64,320]{1,0:T(8,128)(2,1)S(1)}, u32[]{:S(2)}, u32[]{:S(2)}) %collective-permute-start.9) | collective-permute-done | bytes 40992 | tf_op jit(solution)/shard_map/ppermute | solution.py:79
  80.6 22.9 %all_gather.9 = bf16[1024,320]{1,0:T(8,128)(2,1)S(1)} all-gather(bf16[64,320]{1,0:T(8,128)(2,1)S(1)} %convolution_convert_fusion.4), channel_id=1, replica_groups=mesh['groups'=2,'seq'=16] {'seq'}, dimensions={0}, use_global_device_ids=true | all-gather | bytes 696320 | tf_op jit(solution)/shard_map/all_gather | solution.py:84
  105.0 4.7 %collective-permute-done.11 = bf16[64,320]{1,0:T(8,128)(2,1)S(1)} collective-permute-done((bf16[64,320]{1,0:T(8,128)(2,1)S(1)}, bf16[64,320]{1,0:T(8,128)(2,1)S(1)}, u32[]{:S(2)}, u32[]{:S(2)}) %collective-permute-start.11) | collective-permute-done | bytes 40992 | tf_op jit(solution)/shard_map/ppermute | solution.py:79
  109.8 7.4 %collective-permute-done.12 = bf16[64,320]{1,0:T(8,128)(2,1)S(1)} collective-permute-done((bf16[64,320]{1,0:T(8,128)(2,1)S(1)}, bf16[64,320]{1,0:T(8,128)(2,1)S(1)}, u32[]{:S(2)}, u32[]{:S(2)}) %collective-permute-start.12) | collective-permute-done | bytes 40992 | tf_op jit(solution)/shard_map/ppermute | solution.py:79
  118.8 5.6 %collective-permute-done.13 = bf16[64,320]{1,0:T(8,128)(2,1)S(1)} collective-permute-done((bf16[64,320]{1,0:T(8,128)(2,1)S(1)}, bf16[64,320]{1,0:T(8,128)(2,1)S(1)}, u32[]{:S(2)}, u32[]{:S(2)}) %collective-permute-start.13) | collective-permute-done | bytes 40992 | tf_op jit(solution)/shard_map/ppermute | solution.py:79
  142.4 5.6 %copy.55 = bf16[5,8,16,8,512]{4,3,1,0,2:T(8,128)(2,1)} copy(bf16[5,8,16,8,512]{4,3,2,1,0:T(8,128)(2,1)} %bitcast.80) | data formatting | bytes 10485760 | tf_op jit(solution)/shard_map/reshape | solution.py:111
  148.0 5.6 %copy.56 = bf16[5,8,16,8,512]{4,3,1,0,2:T(8,128)(2,1)} copy(bf16[5,8,16,8,512]{4,3,2,1,0:T(8,128)(2,1)} %bitcast.81) | data formatting | bytes 10485760 | tf_op jit(solution)/shard_map/reshape | solution.py:110
  153.6 119.0 %while.18 = (s32[]{:T(128)}, f32[5,512]{1,0:T(8,128)S(1)}, f32[5,512]{1,0:T(8,128)S(1)}, f32[5,512,64]{1,2,0:T(8,128)S(1)}, s32[16]{0:T(128)S(1)}, /*index=5*/bf...) while((s32[]{:T(128)}, f32[5,512]{1,0:T(8,128)S(1)}, ...), condition=%wide.region_5.6_spmd.clone, body=%wide.region_2.5_spmd.clone.sunk | while | flops 384700416 | bytes 19313812 | solution.py:117
  158.5 2.5 fusion.83
  165.9 2.5 fusion.83
  173.3 2.5 fusion.83
  180.8 2.5 fusion.83
  188.2 2.5 fusion.83
  195.7 2.5 fusion.83
  203.1 2.5 fusion.83
  (230 shorter events, 118.6 us)
Async XLA Ops:
  6.5 1.0 copy-start
  6.5 135.9 %all-gather.5.cloned.1.call-start = ((), (), s32[]{:S(2)}) async-start(), calls=%async_computation.1 | async-start | bytes 5570560 | tf_op jit(solution)/shard_map/all_gather | solution.py:102
  9.6 138.4 %all-gather.3.cloned.1.call-start = ((), (), s32[]{:S(2)}) async-start(), calls=%async_computation | async-start | bytes 5570560 | tf_op jit(solution)/shard_map/all_gather | solution.py:101
  12.8 7.3 %collective-permute-start = (bf16[64,320]{1,0:T(8,128)(2,1)S(1)}, bf16[64,320]{1,0:T(8,128)(2,1)S(1)}, u32[]{:S(2)}, u32[]{:S(2)}) collective-permute-start(bf16[64,320]{1,0:T(8,128)(2,1)S(1)} %convolution_convert_fusion.5), channel_id=1, source_target_pairs={{0,1},{1,2},{2,3},{3,4},{4,5},{5,6},{6,7},{7,8},{8,9},{9,10},{10,1... | collective-permute-start | bytes 122888 | tf_op jit(solution)/shard_map/ppermute | solution.py:79
  20.1 6.8 %collective-permute-start.1 = (bf16[64,320]{1,0:T(8,128)(2,1)S(1)}, bf16[64,320]{1,0:T(8,128)(2,1)S(1)}, u32[]{:S(2)}, u32[]{:S(2)}) collective-permute-start(bf16[64,320]{1,0:T(8,128)(2,1)S(1)} %collective-permute-done), channel_id=1, source_target_pairs={{0,1},{1,2},{2,3},{3,4},{4,5},{5,6},{6,7},{7,8},{8,9},{9,10},{10,1... | collective-permute-start | bytes 122888 | tf_op jit(solution)/shard_map/ppermute | solution.py:79
  27.0 7.1 %collective-permute-start.2 = (bf16[64,320]{1,0:T(8,128)(2,1)S(1)}, bf16[64,320]{1,0:T(8,128)(2,1)S(1)}, u32[]{:S(2)}, u32[]{:S(2)}) collective-permute-start(bf16[64,320]{1,0:T(8,128)(2,1)S(1)} %collective-permute-done.1), channel_id=1, source_target_pairs={{0,1},{1,2},{2,3},{3,4},{4,5},{5,6},{6,7},{7,8},{8,9},{9,10},{10,1... | collective-permute-start | bytes 122888 | tf_op jit(solution)/shard_map/ppermute | solution.py:79
  34.0 6.2 %collective-permute-start.3 = (bf16[64,320]{1,0:T(8,128)(2,1)S(1)}, bf16[64,320]{1,0:T(8,128)(2,1)S(1)}, u32[]{:S(2)}, u32[]{:S(2)}) collective-permute-start(bf16[64,320]{1,0:T(8,128)(2,1)S(1)} %collective-permute-done.2), channel_id=1, source_target_pairs={{0,1},{1,2},{2,3},{3,4},{4,5},{5,6},{6,7},{7,8},{8,9},{9,10},{10,1... | collective-permute-start | bytes 122888 | tf_op jit(solution)/shard_map/ppermute | solution.py:79
  40.2 6.2 %collective-permute-start.4 = (bf16[64,320]{1,0:T(8,128)(2,1)S(1)}, bf16[64,320]{1,0:T(8,128)(2,1)S(1)}, u32[]{:S(2)}, u32[]{:S(2)}) collective-permute-start(bf16[64,320]{1,0:T(8,128)(2,1)S(1)} %collective-permute-done.3), channel_id=1, source_target_pairs={{0,1},{1,2},{2,3},{3,4},{4,5},{5,6},{6,7},{7,8},{8,9},{9,10},{10,1... | collective-permute-start | bytes 122888 | tf_op jit(solution)/shard_map/ppermute | solution.py:79
  46.4 7.4 %collective-permute-start.5 = (bf16[64,320]{1,0:T(8,128)(2,1)S(1)}, bf16[64,320]{1,0:T(8,128)(2,1)S(1)}, u32[]{:S(2)}, u32[]{:S(2)}) collective-permute-start(bf16[64,320]{1,0:T(8,128)(2,1)S(1)} %collective-permute-done.4), channel_id=1, source_target_pairs={{0,1},{1,2},{2,3},{3,4},{4,5},{5,6},{6,7},{7,8},{8,9},{9,10},{10,1... | collective-permute-start | bytes 122888 | tf_op jit(solution)/shard_map/ppermute | solution.py:79
  53.8 7.1 %collective-permute-start.6 = (bf16[64,320]{1,0:T(8,128)(2,1)S(1)}, bf16[64,320]{1,0:T(8,128)(2,1)S(1)}, u32[]{:S(2)}, u32[]{:S(2)}) collective-permute-start(bf16[64,320]{1,0:T(8,128)(2,1)S(1)} %collective-permute-done.5), channel_id=1, source_target_pairs={{0,1},{1,2},{2,3},{3,4},{4,5},{5,6},{6,7},{7,8},{8,9},{9,10},{10,1... | collective-permute-start | bytes 122888 | tf_op jit(solution)/shard_map/ppermute | solution.py:79
  60.9 7.2 %collective-permute-start.7 = (bf16[64,320]{1,0:T(8,128)(2,1)S(1)}, bf16[64,320]{1,0:T(8,128)(2,1)S(1)}, u32[]{:S(2)}, u32[]{:S(2)}) collective-permute-start(bf16[64,320]{1,0:T(8,128)(2,1)S(1)} %collective-permute-done.6), channel_id=1, source_target_pairs={{0,1},{1,2},{2,3},{3,4},{4,5},{5,6},{6,7},{7,8},{8,9},{9,10},{10,1... | collective-permute-start | bytes 122888 | tf_op jit(solution)/shard_map/ppermute | solution.py:79
  68.2 6.2 %collective-permute-start.8 = (bf16[64,320]{1,0:T(8,128)(2,1)S(1)}, bf16[64,320]{1,0:T(8,128)(2,1)S(1)}, u32[]{:S(2)}, u32[]{:S(2)}) collective-permute-start(bf16[64,320]{1,0:T(8,128)(2,1)S(1)} %collective-permute-done.7), channel_id=1, source_target_pairs={{0,1},{1,2},{2,3},{3,4},{4,5},{5,6},{6,7},{7,8},{8,9},{9,10},{10,1... | collective-permute-start | bytes 122888 | tf_op jit(solution)/shard_map/ppermute | solution.py:79
  74.4 6.2 %collective-permute-start.9 = (bf16[64,320]{1,0:T(8,128)(2,1)S(1)}, bf16[64,320]{1,0:T(8,128)(2,1)S(1)}, u32[]{:S(2)}, u32[]{:S(2)}) collective-permute-start(bf16[64,320]{1,0:T(8,128)(2,1)S(1)} %collective-permute-done.8), channel_id=1, source_target_pairs={{0,1},{1,2},{2,3},{3,4},{4,5},{5,6},{6,7},{7,8},{8,9},{9,10},{10,1... | collective-permute-start | bytes 122888 | tf_op jit(solution)/shard_map/ppermute | solution.py:79
  80.6 23.0 %collective-permute-start.10 = (bf16[64,320]{1,0:T(8,128)(2,1)S(1)}, bf16[64,320]{1,0:T(8,128)(2,1)S(1)}, u32[]{:S(2)}, u32[]{:S(2)}) collective-permute-start(bf16[64,320]{1,0:T(8,128)(2,1)S(1)} %collective-permute-done.9), channel_id=1, source_target_pairs={{0,1},{1,2},{2,3},{3,4},{4,5},{5,6},{6,7},{7,8},{8,9},{9,10},{10,1... | collective-permute-start | bytes 122888 | tf_op jit(solution)/shard_map/ppermute | solution.py:79
  103.6 6.2 %collective-permute-start.11 = (bf16[64,320]{1,0:T(8,128)(2,1)S(1)}, bf16[64,320]{1,0:T(8,128)(2,1)S(1)}, u32[]{:S(2)}, u32[]{:S(2)}) collective-permute-start(bf16[64,320]{1,0:T(8,128)(2,1)S(1)} %collective-permute-done.10), channel_id=1, source_target_pairs={{0,1},{1,2},{2,3},{3,4},{4,5},{5,6},{6,7},{7,8},{8,9},{9,10},{10,1... | collective-permute-start | bytes 122888 | tf_op jit(solution)/shard_map/ppermute | solution.py:79
  109.8 7.4 %collective-permute-start.12 = (bf16[64,320]{1,0:T(8,128)(2,1)S(1)}, bf16[64,320]{1,0:T(8,128)(2,1)S(1)}, u32[]{:S(2)}, u32[]{:S(2)}) collective-permute-start(bf16[64,320]{1,0:T(8,128)(2,1)S(1)} %collective-permute-done.11), channel_id=1, source_target_pairs={{0,1},{1,2},{2,3},{3,4},{4,5},{5,6},{6,7},{7,8},{8,9},{9,10},{10,1... | collective-permute-start | bytes 122888 | tf_op jit(solution)/shard_map/ppermute | solution.py:79
  117.2 7.2 %collective-permute-start.13 = (bf16[64,320]{1,0:T(8,128)(2,1)S(1)}, bf16[64,320]{1,0:T(8,128)(2,1)S(1)}, u32[]{:S(2)}, u32[]{:S(2)}) collective-permute-start(bf16[64,320]{1,0:T(8,128)(2,1)S(1)} %collective-permute-done.12), channel_id=1, source_target_pairs={{0,1},{1,2},{2,3},{3,4},{4,5},{5,6},{6,7},{7,8},{8,9},{9,10},{10,1... | collective-permute-start | bytes 122888 | tf_op jit(solution)/shard_map/ppermute | solution.py:79
  124.4 10.4 %collective-permute-start.14 = (bf16[64,320]{1,0:T(8,128)(2,1)S(1)}, bf16[64,320]{1,0:T(8,128)(2,1)S(1)}, u32[]{:S(2)}, u32[]{:S(2)}) collective-permute-start(bf16[64,320]{1,0:T(8,128)(2,1)S(1)} %collective-permute-done.13), channel_id=1, source_target_pairs={{0,1},{1,2},{2,3},{3,4},{4,5},{5,6},{6,7},{7,8},{8,9},{9,10},{10,1... | collective-permute-start | bytes 122888 | tf_op jit(solution)/shard_map/ppermute | solution.py:79
  153.6 119.0 %copy-start.1 = (bf16[320,320]{1,0:T(8,128)(2,1)S(1)}, bf16[320,320]{1,0:T(8,128)(2,1)}, u32[]{:S(2)}) copy-start(bf16[320,320]{1,0:T(8,128)(2,1)} %param.17) | copy-start | bytes 614404
Sparse Core Ops, SparseCore 0:
  9.7 64.7 all-gather.4
  76.6 61.9 all-gather.2
